TPU v7x, 128 devices: a whole 4x4x4 slice. The times are simulated.
128 devices in a mesh: mem: 4 (over x_hi, core), tile: 32 (over x_lo, y, z).
Axes of the slice: x: 4 (x_hi: 2, x_lo: 2; x = x_hi * 2 + x_lo), y: 4, z: 4, core: 2. Of those that a mesh axis runs over, the one named last changes fastest.
Arguments:
- latents: float32 [24, 256], P('mem'), may hold values from -6 to 6
- basis: bfloat16 [256, 2, 512, 512], P(None, None, 'tile'), may hold values from -0.375 to 0.375
- conv_in: bfloat16 [9, 64], replicated, may hold values from -2 to 2
- conv_mid: bfloat16 [9, 64, 64], replicated, may hold values from -0.25 to 0.25
- conv_out: bfloat16 [64], replicated, may hold values from -0.75 to 0.75
- pressure_prev: float32 [2, 512, 512], P(None, 'tile'), may hold values from -6 to 6
- source: float32 [2, 512, 512], P(None, 'tile'), may hold values from -6 to 6
- perf_cells: int32 [384, 8], replicated, may hold values from 0 to 524287
- perf_count: int32 [384], replicated, may hold values from 1 to 8
- obs_perturbed: float32 [24, 384], replicated, may hold values from -6 to 6
- obs_error: float32 [384], replicated, may hold values from 0.2 to 2
Outputs:
- pressure: float32 [24, 2, 512, 512], P(None, None, 'tile', 'mem')
- well_data: float32 [24, 384], replicated
- latents_new: float32 [24, 256], P('mem')
All inputs are finite; a program needn't handle non-finite values.
Results may differ from a plain program's by a relative error of at most 0.0055.
Values may be sent and summed in bfloat16 or wider, within the bound.
A program may use at most 128 MiB of HBM per device.

v0:
```python
import math
import jax
import jax.numpy as jnp
from jax import lax
from jax.sharding import PartitionSpec as P

SWEEPS = 2
storage_coef = 1.0


def extended(cells, sides, width):
    for axis, dim in sides:
        count = lax.axis_size(axis)
        ends = count - 1
        head = lax.slice_in_dim(cells, 0, width, axis=dim)
        tail = lax.slice_in_dim(cells, cells.shape[dim] - width, cells.shape[dim], axis=dim)
        cells = jnp.concatenate(
            [
                lax.ppermute(tail, axis, [(i, (i + 1) % count) for i in range(ends)]),
                cells,
                lax.ppermute(head, axis, [((i + 1) % count, i) for i in range(ends)]),
            ],
            axis=dim,
        )
    return cells


def lift(field, conv_in):
    rows = field.shape[1] - 2
    width = field.shape[2]
    padded = jnp.pad(field, ((0, 0), (0, 0), (1, 1)))
    total = jnp.zeros((field.shape[0], conv_in.shape[1], rows, width), jnp.float32)
    for tap in range(9):
        part = padded[:, tap // 3 : tap // 3 + rows, tap % 3 : tap % 3 + width]
        total = total + conv_in[tap].astype(jnp.float32)[None, :, None, None] * part[:, None]
    return jax.nn.relu(total).astype(jnp.bfloat16)


def mix(lifted, field, conv_mid, conv_out):
    rows = field.shape[1]
    width = field.shape[2]
    padded = jnp.pad(lifted, ((0, 0), (0, 0), (0, 0), (1, 1)))
    total = jnp.zeros((field.shape[0], conv_mid.shape[1], rows, width), jnp.float32)
    for tap in range(9):
        part = padded[:, :, tap // 3 : tap // 3 + rows, tap % 3 : tap % 3 + width]
        total = total + jnp.einsum(
            "oc,zcxy->zoxy", conv_mid[tap], part, preferred_element_type=jnp.float32
        )
    deep = jax.nn.relu(total)
    return field + jnp.einsum("c,zcxy->zxy", conv_out.astype(jnp.float32), deep)


def neighbours(wide):
    zpad = jnp.pad(wide, ((0, 0), (1, 1), (0, 0), (0, 0)))
    return [
        zpad[:, 1:-1, 2:, 1:-1],
        zpad[:, 1:-1, :-2, 1:-1],
        zpad[:, 1:-1, 1:-1, 2:],
        zpad[:, 1:-1, 1:-1, :-2],
        zpad[:, 2:, 1:-1, 1:-1],
        zpad[:, :-2, 1:-1, 1:-1],
    ]


def well_terms(perm, press, perf_cells, perf_count, row_start, col_start, grid_rows, grid_cols):
    members = perm.shape[0]
    rows = perm.shape[2]
    width = perm.shape[3]
    wells = perf_cells.shape[0]
    slots = perf_cells.shape[1]
    ids = perf_cells.reshape(-1)
    layer_of = ids // (grid_rows * grid_cols)
    rest = ids % (grid_rows * grid_cols)
    row_local = rest // grid_cols - row_start
    col_local = rest % grid_cols - col_start
    inside = (row_local >= 0) & (row_local < rows) & (col_local >= 0) & (col_local < width)
    local_ids = jnp.where(inside, layer_of * rows * width + row_local * width + col_local, 0)
    used = (jnp.arange(slots)[None, :] < perf_count[:, None]).reshape(-1) & inside
    weight = used.astype(jnp.float32)
    perm_at = jnp.take(perm.reshape(members, -1), local_ids, axis=1) * weight[None, :]
    press_at = jnp.take(press.reshape(members, -1), local_ids, axis=1)
    numer = jnp.sum((perm_at * press_at).reshape(members, wells, slots), axis=2)
    weight_sum = jnp.sum(perm_at.reshape(members, wells, slots), axis=2)
    return (numer, weight_sum)


def body(
    latents,
    basis,
    conv_in,
    conv_mid,
    conv_out,
    pressure_prev,
    source,
    perf_cells,
    perf_count,
    obs_perturbed,
    obs_error,
):
    mem_dev = latents.shape[0]
    layers = basis.shape[1]
    rows = basis.shape[2]
    width = basis.shape[3]
    tile_at = lax.axis_index("tile")
    mem_at = lax.axis_index("mem")
    grid_rows = rows * lax.axis_size("tile")
    flat_basis = basis.reshape(basis.shape[0], -1)
    field = jnp.dot(latents.astype(jnp.bfloat16), flat_basis, preferred_element_type=jnp.float32)
    field = field.reshape(mem_dev, layers, rows, width)
    wide = extended(field, (("tile", 2),), 1)
    lifted = lax.map(lambda single: lift(single, conv_in), wide)
    lifted_wide = extended(lifted, (("tile", 3),), 1)
    log_perm = lax.map(lambda pair: mix(pair[0], pair[1], conv_mid, conv_out), (lifted_wide, field))
    base_full = storage_coef * pressure_prev + source
    log_tiles = lax.all_to_all(log_perm, "mem", split_axis=3, concat_axis=0, tiled=True)
    cols = log_tiles.shape[3]
    perm = jnp.exp(log_tiles)
    base = lax.dynamic_slice_in_dim(base_full, mem_at * cols, cols, 2)
    prev_local = lax.dynamic_slice_in_dim(pressure_prev, mem_at * cols, cols, 2)
    perm_wide = extended(perm, (("mem", 3), ("tile", 2)), 1)
    conduct = [2.0 * perm * other / (perm + other) for other in neighbours(perm_wide)]
    denom = storage_coef + sum(conduct)
    press = jnp.broadcast_to(prev_local, perm.shape)
    for sweep in range(SWEEPS):
        press_wide = extended(press, (("mem", 3), ("tile", 2)), 1)
        acc = base[None] + sum((cval * nval for cval, nval in zip(conduct, neighbours(press_wide))))
        press = acc / denom
    numer, weight_sum = well_terms(
        perm,
        press,
        perf_cells,
        perf_count,
        tile_at * rows,
        mem_at * cols,
        grid_rows,
        cols * lax.axis_size("mem"),
    )
    members = press.shape[0]
    numer, weight_sum = lax.psum((numer, weight_sum), ("mem", "tile"))
    well_data = numer / weight_sum
    scale = 2.0 * obs_error
    centred = well_data - jnp.mean(well_data, axis=0, keepdims=True)
    scaled = centred / (math.sqrt(members - 1) * scale[None, :])
    innov = (obs_perturbed - well_data) / scale[None, :]
    gram = jnp.eye(members, dtype=jnp.float32) + jnp.dot(
        scaled, scaled.T, precision=lax.Precision.HIGHEST
    )
    cross = jnp.dot(scaled, innov.T, precision=lax.Precision.HIGHEST)
    factor = jnp.linalg.cholesky(gram)
    weights = jax.scipy.linalg.cho_solve((factor, True), cross)
    every = lax.all_gather(latents, "mem", axis=0, tiled=True)
    spread = (every - jnp.mean(every, axis=0, keepdims=True)) / math.sqrt(members - 1)
    own_weights = lax.dynamic_slice_in_dim(weights, mem_at * mem_dev, mem_dev, 1)
    latents_new = latents + jnp.dot(own_weights.T, spread, precision=lax.Precision.HIGHEST)
    return (press, well_data, latents_new)


def solution(mesh):
    return jax.shard_map(
        body,
        mesh=mesh,
        in_specs=(
            P("mem", None),
            P(None, None, "tile", None),
            P(),
            P(),
            P(),
            P(None, "tile", None),
            P(None, "tile", None),
            P(),
            P(),
            P(),
            P(),
        ),
        out_specs=(P(None, None, "tile", "mem"), P(), P("mem", None)),
        check_vma=False,
    )
```

profile of v0, /device:TPU:1, one launch (start us, length us, event | category | flops | bytes accessed | tf_op | source)
XLA Modules:
  0.0 651.2 jit_solution(13168219996132069656)
XLA Ops:
  7.2 15.4 %copy.59 = bf16[32,8,32,512]{3,1,2,0:T(8,128)(2,1)} copy(bf16[32,8,32,512]{3,2,1,0:T(8,128)(2,1)} %bitcast.226) | data formatting | bytes 16777216
  22.6 11.9 %copy.29 = bf16[16384,256]{1,0:T(8,128)(2,1)} copy(bf16[16384,256]{0,1:T(8,128)(2,1)} %bitcast.222) | data formatting | bytes 16777216 | tf_op jit(solution)/shard_map/dot_general | solution.py:108
  34.5 5.6 fusion.110
  49.4 35.6 %while.24 = (s32[]{:T(128)}, bf16[6,2,64,16,512]{4,2,3,1,0:T(8,128)(2,1)}, bf16[9,64]{1,0:T(8,128)(2,1)S(1)}, f32[6,2,18,512]{3,0,2,1:T(8,128)S(1)}, s32[]{:T(128)}) while((s32[]{:T(128)}, bf16[6,2,64,16,512]{4,2,3,1,0:T(8,128)(2,1)}, bf16[9,64]{1,0:T(8,128)(2,1)S(1)}, f32[6,2,18,512]{3,0,2,1:T(8,128)S(1)}, s32[]{:T(128)}) %tuple.105), condition=%wide.region_1.2_spmd, body=%wide.region_0.1_spmd.sunk | while | flops 19923520 | bytes 8067265 | solution.py:111
  93.6 6.9 %collective-permute-start.7 = (f32[24,2,16,1]{3,2,1,0:T(8,128)}, f32[24,2,16,1]{3,2,1,0:T(8,128)}, u32[]{:S(2)}, u32[]{:S(2)}) collective-permute-start(f32[24,2,16,1]{3,2,1,0:T(8,128)} %broadcast_in_dim.48), channel_id=1, source_target_pairs={{0,32},{32,64},{64,96},{1,33},{33,65},{65,97},{2,34},{34,66},{66,9... | collective-permute-start | bytes 9224 | tf_op jit(solution)/shard_map/ppermute | solution.py:19
  110.0 10.3 %pad_maximum_fusion = bf16[6,2,64,18,512]{4,2,3,1,0:T(8,128)(2,1)} fusion(bf16[6,2,64,1,512]{4,2,3,1,0:T(8,128)(2,1)S(1)} %collective-permute-done.3, bf16[6,2,64,16,512]{4,2,3,1,0:T(8,128)(2,1)} %get-tuple-element.134, bf16[6,2,64,1,512]{4,2,3,1,0:T(8,128)(2,1)S(1)} %collective-permute-done.2), kind=kLoop, calls=%fused_computation.83 | loop fusion | flops 14155776 | bytes 28311552 | tf_op jit(solution)/shard_map/concatenate | solution.py:17
  120.3 224.6 %while.25 = (s32[]{:T(128)}, f32[6,2,16,512]{3,2,1,0:T(8,128)S(1)}, f32[6,2,16,512]{3,0,2,1:T(8,128)S(1)}, bf16[6,2,64,18,512]{4,2,3,1,0:T(8,128)(2,1)}, bf16[9,...) while((s32[]{:T(128)}, f32[6,2,16,512]{3,2,1,0:T(8,128)S(1)}, ...), condition=%wide.region_3.4_spmd, body=%wide.region_2.3_spmd.sunk | while | flops 1219510272 | bytes 92815952 | solution.py:113
  144.2 13.4 %fusion.170 = f32[1,2,16,512]{3,0,2,1:T(1,128)S(1)} fusion(f32[2,16,512,64]{2,3,1,0:T(8,128)} %fusion.162, f32[2,16,512,64]{2,3,1,0:T(8,128)} %fusion.163, f32[2,16,512,64]{2,3,1,0:T(8,128)} %fusion.164, f32[2,16,512,64]{2,3,1,0:T(8,128)} %fusion.165, f32[2,16,512,64]{2,3,1,0:T(8,128)} %fusion.166, f32[2,16,512,64]{2,3,1,0:T(8,128)} %fusion.167, ...), kind=kOutput, calls=%fused_computation.21.clone.1 | convolution fusion | flops 145752064 | bytes 35996160 | tf_op jit(solution)/shard_map/while/body/eval_jaxpr/c,zcxy->zxy/dot_general | solution.py:50
  181.7 13.4 %fusion.170 = f32[1,2,16,512]{3,0,2,1:T(1,128)S(1)} fusion(f32[2,16,512,64]{2,3,1,0:T(8,128)} %fusion.162, f32[2,16,512,64]{2,3,1,0:T(8,128)} %fusion.163, f32[2,16,512,64]{2,3,1,0:T(8,128)} %fusion.164, f32[2,16,512,64]{2,3,1,0:T(8,128)} %fusion.165, f32[2,16,512,64]{2,3,1,0:T(8,128)} %fusion.166, f32[2,16,512,64]{2,3,1,0:T(8,128)} %fusion.167, ...), kind=kOutput, calls=%fused_computation.21.clone.1 | convolution fusion | flops 145752064 | bytes 35996160 | tf_op jit(solution)/shard_map/while/body/eval_jaxpr/c,zcxy->zxy/dot_general | solution.py:50
  219.1 13.4 %fusion.170 = f32[1,2,16,512]{3,0,2,1:T(1,128)S(1)} fusion(f32[2,16,512,64]{2,3,1,0:T(8,128)} %fusion.162, f32[2,16,512,64]{2,3,1,0:T(8,128)} %fusion.163, f32[2,16,512,64]{2,3,1,0:T(8,128)} %fusion.164, f32[2,16,512,64]{2,3,1,0:T(8,128)} %fusion.165, f32[2,16,512,64]{2,3,1,0:T(8,128)} %fusion.166, f32[2,16,512,64]{2,3,1,0:T(8,128)} %fusion.167, ...), kind=kOutput, calls=%fused_computation.21.clone.1 | convolution fusion | flops 145752064 | bytes 35996160 | tf_op jit(solution)/shard_map/while/body/eval_jaxpr/c,zcxy->zxy/dot_general | solution.py:50
  256.6 13.4 %fusion.170 = f32[1,2,16,512]{3,0,2,1:T(1,128)S(1)} fusion(f32[2,16,512,64]{2,3,1,0:T(8,128)} %fusion.162, f32[2,16,512,64]{2,3,1,0:T(8,128)} %fusion.163, f32[2,16,512,64]{2,3,1,0:T(8,128)} %fusion.164, f32[2,16,512,64]{2,3,1,0:T(8,128)} %fusion.165, f32[2,16,512,64]{2,3,1,0:T(8,128)} %fusion.166, f32[2,16,512,64]{2,3,1,0:T(8,128)} %fusion.167, ...), kind=kOutput, calls=%fused_computation.21.clone.1 | convolution fusion | flops 145752064 | bytes 35996160 | tf_op jit(solution)/shard_map/while/body/eval_jaxpr/c,zcxy->zxy/dot_general | solution.py:50
  294.0 13.4 %fusion.170 = f32[1,2,16,512]{3,0,2,1:T(1,128)S(1)} fusion(f32[2,16,512,64]{2,3,1,0:T(8,128)} %fusion.162, f32[2,16,512,64]{2,3,1,0:T(8,128)} %fusion.163, f32[2,16,512,64]{2,3,1,0:T(8,128)} %fusion.164, f32[2,16,512,64]{2,3,1,0:T(8,128)} %fusion.165, f32[2,16,512,64]{2,3,1,0:T(8,128)} %fusion.166, f32[2,16,512,64]{2,3,1,0:T(8,128)} %fusion.167, ...), kind=kOutput, calls=%fused_computation.21.clone.1 | convolution fusion | flops 145752064 | bytes 35996160 | tf_op jit(solution)/shard_map/while/body/eval_jaxpr/c,zcxy->zxy/dot_general | solution.py:50
  331.4 13.4 %fusion.170 = f32[1,2,16,512]{3,0,2,1:T(1,128)S(1)} fusion(f32[2,16,512,64]{2,3,1,0:T(8,128)} %fusion.162, f32[2,16,512,64]{2,3,1,0:T(8,128)} %fusion.163, f32[2,16,512,64]{2,3,1,0:T(8,128)} %fusion.164, f32[2,16,512,64]{2,3,1,0:T(8,128)} %fusion.165, f32[2,16,512,64]{2,3,1,0:T(8,128)} %fusion.166, f32[2,16,512,64]{2,3,1,0:T(8,128)} %fusion.167, ...), kind=kOutput, calls=%fused_computation.21.clone.1 | convolution fusion | flops 145752064 | bytes 35996160 | tf_op jit(solution)/shard_map/while/body/eval_jaxpr/c,zcxy->zxy/dot_general | solution.py:50
  347.0 5.0 reshape.341
  352.0 7.6 %all-to-all-start = ((f32[4,1,24576]{2,1,0:T(1,128)}), f32[4,1,24576]{2,1,0:T(1,128)S(1)}, u32[]{:S(2)}, u32[]{:S(2)}) async-start(f32[4,1,24576]{2,1,0:T(1,128)} %reshape.341), calls=%async_computation | async-start | bytes 786432 | tf_op jit(solution)/shard_map/all_to_all | solution.py:115
  361.8 5.9 all-to-all-done
  404.6 4.8 fusion.71
  409.5 5.6 collective-permute-start.12
  419.8 5.9 collective-permute-done.13
  431.7 5.8 all-gather
  440.0 10.8 %gather_fusion = f32[3072,24]{1,0:T(8,128)} fusion(f32[24,4096]{0,1:T(8,128)S(1)} %copy.38, s32[3072]{0:T(1024)S(1)} %broadcast_clamp_fusion), kind=kCustom, calls=%fused_computation.clone | custom fusion | bytes 602112 | tf_op jit(solution)/shard_map/jit(_take)/gather | solution.py:80
  456.5 10.8 %gather_fusion.1 = f32[3072,24]{1,0:T(8,128)} fusion(f32[24,4096]{0,1:T(8,128)S(1)} %bitcast.225, s32[3072]{0:T(1024)S(1)} %broadcast_clamp_fusion), kind=kCustom, calls=%fused_computation.1.clone | custom fusion | bytes 602112 | tf_op jit(solution)/shard_map/jit(_take)/gather | solution.py:81
  467.4 4.6 bitcast_reduce_fusion
  472.2 161.6 %all-reduce.8.cloned.1.call-done = (f32[24,384]{0,1:T(8,128)}, f32[24,384]{0,1:T(8,128)}) async-done(((f32[24,384]{0,1:T(8,128)}, f32[24,384]{0,1:T(8,128)}), (f32[24,384]{0,1:T(8,128)}, f32[24,384]{0,1:T(8,128)})) %all-reduce.8.cloned.1.call-update) | async-done | bytes 73744 | tf_op jit(solution)/shard_map/psum | solution.py:139
  (239 shorter events, 276.3 us)
Async XLA Ops:
  40.1 5.9 collective-permute-start
  44.5 4.8 collective-permute-start.1
  85.1 18.2 %copy-start.22 = (s32[384,8]{0,1:T(8,128)S(1)}, s32[384,8]{0,1:T(8,128)}, u32[]{:S(2)}) copy-start(s32[384,8]{0,1:T(8,128)} %param.24) | copy-start | bytes 36868
  85.1 19.1 %copy-start.24 = (s32[384]{0:T(512)S(1)}, s32[384]{0:T(512)}, u32[]{:S(2)}) copy-start(s32[384]{0:T(512)} %param.25) | copy-start | bytes 4612
  87.8 18.4 %collective-permute-start.2 = (bf16[6,2,64,1,512]{4,2,3,1,0:T(8,128)(2,1)}, bf16[6,2,64,1,512]{4,2,3,1,0:T(8,128)(2,1)S(1)}, u32[]{:S(2)}, u32[]{:S(2)}) collective-permute-start(bf16[6,2,64,1,512]{4,2,3,1,0:T(8,128)(2,1)} %get-tuple-element.220), channel_id=1, source_target_pairs={{0,1},{1,2},{2,3},{3,4},{4,5},{5,6},{6,7},{7,8},{8,9},{9,10},{10,1... | collective-permute-start | bytes 2359304 | tf_op jit(solution)/shard_map/ppermute | solution.py:19
  91.2 18.8 %collective-permute-start.3 = (bf16[6,2,64,1,512]{4,2,3,1,0:T(8,128)(2,1)}, bf16[6,2,64,1,512]{4,2,3,1,0:T(8,128)(2,1)S(1)}, u32[]{:S(2)}, u32[]{:S(2)}) collective-permute-start(bf16[6,2,64,1,512]{4,2,3,1,0:T(8,128)(2,1)} %get-tuple-element.221), channel_id=1, source_target_pairs={{1,0},{2,1},{3,2},{4,3},{5,4},{6,5},{7,6},{8,7},{9,8},{10,9},{11,1... | collective-permute-start | bytes 2359304 | tf_op jit(solution)/shard_map/ppermute | solution.py:21
  93.6 292.5 %collective-permute-start.7 = (f32[24,2,16,1]{3,2,1,0:T(8,128)}, f32[24,2,16,1]{3,2,1,0:T(8,128)}, u32[]{:S(2)}, u32[]{:S(2)}) collective-permute-start(f32[24,2,16,1]{3,2,1,0:T(8,128)} %broadcast_in_dim.48), channel_id=1, source_target_pairs={{0,32},{32,64},{64,96},{1,33},{33,65},{65,97},{2,34},{34,66},{66,9... | collective-permute-start | bytes 9224 | tf_op jit(solution)/shard_map/ppermute | solution.py:19
  101.3 284.8 %collective-permute-start.8 = (f32[24,2,16,1]{3,2,1,0:T(8,128)}, f32[24,2,16,1]{3,2,1,0:T(8,128)}, u32[]{:S(2)}, u32[]{:S(2)}) collective-permute-start(f32[24,2,16,1]{3,2,1,0:T(8,128)} %broadcast_in_dim.50), channel_id=1, source_target_pairs={{32,0},{64,32},{96,64},{33,1},{65,33},{97,65},{34,2},{66,34},{98,6... | collective-permute-start | bytes 9224 | tf_op jit(solution)/shard_map/ppermute | solution.py:21
  105.0 15.3 %copy-start.20 = (bf16[64]{0:T(256)(128)(2,1)S(1)}, bf16[64]{0:T(256)(128)(2,1)}, u32[]{:S(2)}) copy-start(bf16[64]{0:T(256)(128)(2,1)} %param.21) | copy-start | bytes 388
  352.0 15.7 %all-to-all-start = ((f32[4,1,24576]{2,1,0:T(1,128)}), f32[4,1,24576]{2,1,0:T(1,128)S(1)}, u32[]{:S(2)}, u32[]{:S(2)}) async-start(f32[4,1,24576]{2,1,0:T(1,128)} %reshape.341), calls=%async_computation | async-start | bytes 786432 | tf_op jit(solution)/shard_map/all_to_all | solution.py:115
  359.6 274.3 %all-reduce.8.cloned.1.call-start = ((), (), s32[]{:S(2)}) async-start(), calls=%async_computation.1 | async-start | bytes 786432 | tf_op jit(solution)/shard_map/psum | solution.py:139
  381.4 11.5 %collective-permute-start.4 = (f32[24,2,16,1]{3,2,1,0:T(8,128)S(1)}, f32[24,2,16,1]{3,2,1,0:T(8,128)S(1)}, u32[]{:S(2)}, u32[]{:S(2)}) collective-permute-start(f32[24,2,16,1]{3,2,1,0:T(8,128)S(1)} %get-tuple-element.232), channel_id=1, source_target_pairs={{0,32},{32,64},{64,96},{1,33},{33,65},{65,97},{2,34},{34,66},{66,9... | collective-permute-start | bytes 9224 | tf_op jit(solution)/shard_map/ppermute | solution.py:19
  384.2 10.6 %collective-permute-start.5 = (f32[24,2,16,1]{3,2,1,0:T(8,128)S(1)}, f32[24,2,16,1]{3,2,1,0:T(8,128)S(1)}, u32[]{:S(2)}, u32[]{:S(2)}) collective-permute-start(f32[24,2,16,1]{3,2,1,0:T(8,128)S(1)} %get-tuple-element.233), channel_id=1, source_target_pairs={{32,0},{64,32},{96,64},{33,1},{65,33},{97,65},{34,2},{66,34},{98,6... | collective-permute-start | bytes 9224 | tf_op jit(solution)/shard_map/ppermute | solution.py:21
  387.8 12.5 %collective-permute-start.11 = (f32[24,2,1,130]{3,2,1,0:T(1,128)S(1)}, f32[24,2,1,130]{3,2,1,0:T(1,128)S(1)}, u32[]{:S(2)}, u32[]{:S(2)}) collective-permute-start(f32[24,2,1,130]{3,2,1,0:T(1,128)S(1)} %get-tuple-element.226), channel_id=1, source_target_pairs={{0,1},{1,2},{2,3},{3,4},{4,5},{5,6},{6,7},{7,8},{8,9},{9,10},{10,1... | collective-permute-start | bytes 74888 | tf_op jit(solution)/shard_map/ppermute | solution.py:19
  391.6 8.7 %collective-permute-start.9 = (f32[24,2,1,130]{3,2,1,0:T(1,128)S(1)}, f32[24,2,1,130]{3,2,1,0:T(1,128)S(1)}, u32[]{:S(2)}, u32[]{:S(2)}) collective-permute-start(f32[24,2,1,130]{3,2,1,0:T(1,128)S(1)} %get-tuple-element.227), channel_id=1, source_target_pairs={{1,0},{2,1},{3,2},{4,3},{5,4},{6,5},{7,6},{8,7},{9,8},{10,9},{11,1... | collective-permute-start | bytes 74888 | tf_op jit(solution)/shard_map/ppermute | solution.py:21
  395.2 6.9 %collective-permute-start.10 = (f32[24,2,1,130]{3,2,1,0:T(1,128)S(1)}, f32[24,2,1,130]{3,2,1,0:T(1,128)S(1)}, u32[]{:S(2)}, u32[]{:S(2)}) collective-permute-start(f32[24,2,1,130]{3,2,1,0:T(1,128)S(1)} %get-tuple-element.224), channel_id=1, source_target_pairs={{0,1},{1,2},{2,3},{3,4},{4,5},{5,6},{6,7},{7,8},{8,9},{9,10},{10,1... | collective-permute-start | bytes 74888 | tf_op jit(solution)/shard_map/ppermute | solution.py:19
  399.0 4.9 collective-permute-start.6
  409.3 22.3 %copy-start.25 = (f32[384]{0:T(512)S(1)}, f32[384]{0:T(512)}, u32[]{:S(2)}) copy-start(f32[384]{0:T(512)} %param.27) | copy-start | bytes 4612
  409.3 22.3 %copy-start.13 = (f32[6,256]{1,0:T(8,128)S(1)}, f32[6,256]{1,0:T(8,128)}, u32[]{:S(2)}) copy-start(f32[6,256]{1,0:T(8,128)} %param.17) | copy-start | bytes 18436
  409.5 10.3 %collective-permute-start.12 = (f32[24,2,16,1]{3,2,1,0:T(8,128)S(1)}, f32[24,2,16,1]{3,2,1,0:T(8,128)S(1)}, u32[]{:S(2)}, u32[]{:S(2)}) collective-permute-start(f32[24,2,16,1]{3,2,1,0:T(8,128)S(1)} %get-tuple-element.230), channel_id=1, source_target_pairs={{0,32},{32,64},{64,96},{1,33},{33,65},{65,97},{2,34},{34,66},{66,9... | collective-permute-start | bytes 9224 | tf_op jit(solution)/shard_map/ppermute | solution.py:19
  415.1 10.6 %collective-permute-start.13 = (f32[24,2,16,1]{3,2,1,0:T(8,128)S(1)}, f32[24,2,16,1]{3,2,1,0:T(8,128)S(1)}, u32[]{:S(2)}, u32[]{:S(2)}) collective-permute-start(f32[24,2,16,1]{3,2,1,0:T(8,128)S(1)} %get-tuple-element.231), channel_id=1, source_target_pairs={{32,0},{64,32},{96,64},{33,1},{65,33},{97,65},{34,2},{66,34},{98,6... | collective-permute-start | bytes 9224 | tf_op jit(solution)/shard_map/ppermute | solution.py:21
  419.8 17.7 %copy-start.4 = (f32[24,2,16,1]{3,2,1,0:T(8,128)}, f32[24,2,16,1]{3,2,1,0:T(8,128)S(1)}, u32[]{:S(2)}) copy-start(f32[24,2,16,1]{3,2,1,0:T(8,128)S(1)} %collective-permute-done.12) | copy-start | bytes 9220
  426.1 24.8 %collective-permute-start.14 = (f32[24,2,1,130]{3,2,1,0:T(1,128)S(1)}, f32[24,2,1,130]{3,2,1,0:T(1,128)S(1)}, u32[]{:S(2)}, u32[]{:S(2)}) collective-permute-start(f32[24,2,1,130]{3,2,1,0:T(1,128)S(1)} %get-tuple-element.223), channel_id=1, source_target_pairs={{1,0},{2,1},{3,2},{4,3},{5,4},{6,5},{7,6},{8,7},{9,8},{10,9},{11,1... | collective-permute-start | bytes 74888 | tf_op jit(solution)/shard_map/ppermute | solution.py:21
  427.4 23.5 %collective-permute-start.15 = (f32[24,2,1,130]{3,2,1,0:T(1,128)S(1)}, f32[24,2,1,130]{3,2,1,0:T(1,128)S(1)}, u32[]{:S(2)}, u32[]{:S(2)}) collective-permute-start(f32[24,2,1,130]{3,2,1,0:T(1,128)S(1)} %get-tuple-element.222), channel_id=1, source_target_pairs={{0,1},{1,2},{2,3},{3,4},{4,5},{5,6},{6,7},{7,8},{8,9},{9,10},{10,1... | collective-permute-start | bytes 74888 | tf_op jit(solution)/shard_map/ppermute | solution.py:19
  (20 other events, 174.6 us)
Sparse Core Ops, SparseCore 0:
  472.2 161.6 all-reduce.7
where the time goes:
time: 660 us; the launch traced here: 651 us
  matrix products  221 us (33%)
  waiting for transfers between devices  188 us (28%)
  local copies, waits for them, and re-layouts  107 us (16%)
  other arithmetic  58.8 us (9%)
  starting transfers between devices  55.2 us (8%)
  between operations  15.1 us (2%)
    psum x1, waiting for transfers between devices, body(): numer, weight_sum = lax.psum((numer, weight_sum), ('mem', 'tile'))  162 us
    dot_general x48, matrix products, mix(): jnp.einsum('oc,zcxy->zoxy', conv_mid[tap], part, preferred_element_type=j...  132 us
    dot_general x6, matrix products, mix(): return field + jnp.einsum('c,zcxy->zxy', conv_out.astype(jnp.float32), deep)  80.6 us
    ppermute x8, starting transfers between devices, extended(): lax.ppermute(tail, axis, [(i, (i + 1) % count) for i in range(ends)])  35 us
    unnamed x59, local copies, waits for them, and re-layouts  25.7 us
    convert_element_type x6, other arithmetic, lift(): return jax.nn.relu(total).astype(jnp.bfloat16)  18.8 us
    concatenate x8, other arithmetic, extended(): jnp.concatenate([lax.ppermute(tail, axis, [(i, (i + 1) % count) for i in...  17 us
    ppermute x8, waiting for transfers between devices, extended(): lax.ppermute(head, axis, [((i + 1) % count, i) for i in range(ends)])  16.6 us
  transfers between devices with their start and end apart: 18, of which 9 were waited for; matrix products, arithmetic and copies ran while one was open for 43% of the time, Pallas kernels for 0%

commit v1 on v0

--- a/solution.py
+++ b/solution.py
@@ -136,7 +136,7 @@
         cols * lax.axis_size("mem"),
     )
     members = press.shape[0]
-    numer, weight_sum = lax.psum((numer, weight_sum), ("mem", "tile"))
+    numer, weight_sum = lax.psum(lax.psum((numer, weight_sum), "mem"), "tile")
     well_data = numer / weight_sum
     scale = 2.0 * obs_error
     centred = well_data - jnp.mean(well_data, axis=0, keepdims=True)

time: 660 us -> 847 us (1.28)
  the two profiles are of different devices: /device:TPU:1 before, /device:TPU:6 now
where the time goes in v1:
time: 847 us; the launch traced here: 838 us
  waiting for transfers between devices  349 us (41%)
  matrix products  221 us (26%)
  local copies, waits for them, and re-layouts  107 us (13%)
  starting transfers between devices  80.1 us (9%)
  other arithmetic  58.4 us (7%)
  between operations  15.1 us (2%)
    psum x2, waiting for transfers between devices, body(): numer, weight_sum = lax.psum(lax.psum((numer, weight_sum), 'mem'), 'tile')  333 us
    dot_general x48, matrix products, mix(): jnp.einsum('oc,zcxy->zoxy', conv_mid[tap], part, preferred_element_type=j...  132 us
    dot_general x6, matrix products, mix(): return field + jnp.einsum('c,zcxy->zxy', conv_out.astype(jnp.float32), deep)  80.6 us
    ppermute x8, starting transfers between devices, extended(): lax.ppermute(head, axis, [((i + 1) % count, i) for i in range(ends)])  55.5 us
    unnamed x53, local copies, waits for them, and re-layouts  25.6 us
    convert_element_type x6, other arithmetic, lift(): return jax.nn.relu(total).astype(jnp.bfloat16)  18.8 us
    ppermute x8, starting transfers between devices, extended(): lax.ppermute(tail, axis, [(i, (i + 1) % count) for i in range(ends)])  17.5 us
    concatenate x8, other arithmetic, extended(): jnp.concatenate([lax.ppermute(tail, axis, [(i, (i + 1) % count) for i in...  17.1 us
  transfers between devices with their start and end apart: 19, of which 8 were waited for; matrix products, arithmetic and copies ran while one was open for 33% of the time, Pallas kernels for 0%

profile of v1, /device:TPU:6, one launch (start us, length us, event | category | flops | bytes accessed | tf_op | source)
XLA Modules:
  0.0 838.4 jit_solution(1512482527280808781)
XLA Ops:
  7.2 15.4 %copy.59 = bf16[32,8,32,512]{3,1,2,0:T(8,128)(2,1)} copy(bf16[32,8,32,512]{3,2,1,0:T(8,128)(2,1)} %bitcast.226) | data formatting | bytes 16777216
  22.6 11.9 %copy.29 = bf16[16384,256]{1,0:T(8,128)(2,1)} copy(bf16[16384,256]{0,1:T(8,128)(2,1)} %bitcast.222) | data formatting | bytes 16777216 | tf_op jit(solution)/shard_map/dot_general | solution.py:108
  34.5 5.6 fusion.110
  44.0 6.9 collective-permute-start.1
  52.4 35.6 %while.24 = (s32[]{:T(128)}, bf16[6,2,64,16,512]{4,2,3,1,0:T(8,128)(2,1)}, bf16[9,64]{1,0:T(8,128)(2,1)S(1)}, f32[6,2,18,512]{3,0,2,1:T(8,128)S(1)}, s32[]{:T(128)}) while((s32[]{:T(128)}, bf16[6,2,64,16,512]{4,2,3,1,0:T(8,128)(2,1)}, bf16[9,64]{1,0:T(8,128)(2,1)S(1)}, f32[6,2,18,512]{3,0,2,1:T(8,128)S(1)}, s32[]{:T(128)}) %tuple.108), condition=%wide.region_1.2_spmd, body=%wide.region_0.1_spmd.sunk | while | flops 19923520 | bytes 8067265 | solution.py:111
  92.6 8.4 %collective-permute-start.3 = (bf16[6,2,64,1,512]{4,2,3,1,0:T(8,128)(2,1)}, bf16[6,2,64,1,512]{4,2,3,1,0:T(8,128)(2,1)S(1)}, u32[]{:S(2)}, u32[]{:S(2)}) collective-permute-start(bf16[6,2,64,1,512]{4,2,3,1,0:T(8,128)(2,1)} %get-tuple-element.223), channel_id=1, source_target_pairs={{1,0},{2,1},{3,2},{4,3},{5,4},{6,5},{7,6},{8,7},{9,8},{10,9},{11,1... | collective-permute-start | bytes 2359304 | tf_op jit(solution)/shard_map/ppermute | solution.py:21
  117.0 10.4 %pad_maximum_fusion = bf16[6,2,64,18,512]{4,2,3,1,0:T(8,128)(2,1)} fusion(bf16[6,2,64,1,512]{4,2,3,1,0:T(8,128)(2,1)S(1)} %collective-permute-done.3, bf16[6,2,64,16,512]{4,2,3,1,0:T(8,128)(2,1)} %get-tuple-element.134, bf16[6,2,64,1,512]{4,2,3,1,0:T(8,128)(2,1)S(1)} %collective-permute-done.2), kind=kLoop, calls=%fused_computation.83 | loop fusion | flops 14155776 | bytes 28311552 | tf_op jit(solution)/shard_map/concatenate | solution.py:17
  127.5 224.5 %while.25 = (s32[]{:T(128)}, f32[6,2,16,512]{3,2,1,0:T(8,128)S(1)}, f32[6,2,16,512]{3,0,2,1:T(8,128)S(1)}, bf16[6,2,64,18,512]{4,2,3,1,0:T(8,128)(2,1)}, bf16[9,...) while((s32[]{:T(128)}, f32[6,2,16,512]{3,2,1,0:T(8,128)S(1)}, ...), condition=%wide.region_3.4_spmd, body=%wide.region_2.3_spmd.sunk | while | flops 1219510272 | bytes 92815952 | solution.py:113
  151.3 13.4 %fusion.170 = f32[1,2,16,512]{3,0,2,1:T(1,128)S(1)} fusion(f32[2,16,512,64]{2,3,1,0:T(8,128)} %fusion.162, f32[2,16,512,64]{2,3,1,0:T(8,128)} %fusion.163, f32[2,16,512,64]{2,3,1,0:T(8,128)} %fusion.164, f32[2,16,512,64]{2,3,1,0:T(8,128)} %fusion.165, f32[2,16,512,64]{2,3,1,0:T(8,128)} %fusion.166, f32[2,16,512,64]{2,3,1,0:T(8,128)} %fusion.167, ...), kind=kOutput, calls=%fused_computation.21.clone.1 | convolution fusion | flops 145752064 | bytes 35996160 | tf_op jit(solution)/shard_map/while/body/eval_jaxpr/c,zcxy->zxy/dot_general | solution.py:50
  188.8 13.4 %fusion.170 = f32[1,2,16,512]{3,0,2,1:T(1,128)S(1)} fusion(f32[2,16,512,64]{2,3,1,0:T(8,128)} %fusion.162, f32[2,16,512,64]{2,3,1,0:T(8,128)} %fusion.163, f32[2,16,512,64]{2,3,1,0:T(8,128)} %fusion.164, f32[2,16,512,64]{2,3,1,0:T(8,128)} %fusion.165, f32[2,16,512,64]{2,3,1,0:T(8,128)} %fusion.166, f32[2,16,512,64]{2,3,1,0:T(8,128)} %fusion.167, ...), kind=kOutput, calls=%fused_computation.21.clone.1 | convolution fusion | flops 145752064 | bytes 35996160 | tf_op jit(solution)/shard_map/while/body/eval_jaxpr/c,zcxy->zxy/dot_general | solution.py:50
  226.2 13.4 %fusion.170 = f32[1,2,16,512]{3,0,2,1:T(1,128)S(1)} fusion(f32[2,16,512,64]{2,3,1,0:T(8,128)} %fusion.162, f32[2,16,512,64]{2,3,1,0:T(8,128)} %fusion.163, f32[2,16,512,64]{2,3,1,0:T(8,128)} %fusion.164, f32[2,16,512,64]{2,3,1,0:T(8,128)} %fusion.165, f32[2,16,512,64]{2,3,1,0:T(8,128)} %fusion.166, f32[2,16,512,64]{2,3,1,0:T(8,128)} %fusion.167, ...), kind=kOutput, calls=%fused_computation.21.clone.1 | convolution fusion | flops 145752064 | bytes 35996160 | tf_op jit(solution)/shard_map/while/body/eval_jaxpr/c,zcxy->zxy/dot_general | solution.py:50
  263.6 13.4 %fusion.170 = f32[1,2,16,512]{3,0,2,1:T(1,128)S(1)} fusion(f32[2,16,512,64]{2,3,1,0:T(8,128)} %fusion.162, f32[2,16,512,64]{2,3,1,0:T(8,128)} %fusion.163, f32[2,16,512,64]{2,3,1,0:T(8,128)} %fusion.164, f32[2,16,512,64]{2,3,1,0:T(8,128)} %fusion.165, f32[2,16,512,64]{2,3,1,0:T(8,128)} %fusion.166, f32[2,16,512,64]{2,3,1,0:T(8,128)} %fusion.167, ...), kind=kOutput, calls=%fused_computation.21.clone.1 | convolution fusion | flops 145752064 | bytes 35996160 | tf_op jit(solution)/shard_map/while/body/eval_jaxpr/c,zcxy->zxy/dot_general | solution.py:50
  301.0 13.4 %fusion.170 = f32[1,2,16,512]{3,0,2,1:T(1,128)S(1)} fusion(f32[2,16,512,64]{2,3,1,0:T(8,128)} %fusion.162, f32[2,16,512,64]{2,3,1,0:T(8,128)} %fusion.163, f32[2,16,512,64]{2,3,1,0:T(8,128)} %fusion.164, f32[2,16,512,64]{2,3,1,0:T(8,128)} %fusion.165, f32[2,16,512,64]{2,3,1,0:T(8,128)} %fusion.166, f32[2,16,512,64]{2,3,1,0:T(8,128)} %fusion.167, ...), kind=kOutput, calls=%fused_computation.21.clone.1 | convolution fusion | flops 145752064 | bytes 35996160 | tf_op jit(solution)/shard_map/while/body/eval_jaxpr/c,zcxy->zxy/dot_general | solution.py:50
  338.5 13.4 %fusion.170 = f32[1,2,16,512]{3,0,2,1:T(1,128)S(1)} fusion(f32[2,16,512,64]{2,3,1,0:T(8,128)} %fusion.162, f32[2,16,512,64]{2,3,1,0:T(8,128)} %fusion.163, f32[2,16,512,64]{2,3,1,0:T(8,128)} %fusion.164, f32[2,16,512,64]{2,3,1,0:T(8,128)} %fusion.165, f32[2,16,512,64]{2,3,1,0:T(8,128)} %fusion.166, f32[2,16,512,64]{2,3,1,0:T(8,128)} %fusion.167, ...), kind=kOutput, calls=%fused_computation.21.clone.1 | convolution fusion | flops 145752064 | bytes 35996160 | tf_op jit(solution)/shard_map/while/body/eval_jaxpr/c,zcxy->zxy/dot_general | solution.py:50
  359.0 6.9 all-to-all-start
  387.5 5.1 collective-permute-start.5
  396.3 8.1 collective-permute-start.9
  406.7 8.1 collective-permute-start.6
  435.1 8.4 %collective-permute-start.14 = (f32[24,2,1,130]{3,2,1,0:T(1,128)S(1)}, f32[24,2,1,130]{3,2,1,0:T(1,128)S(1)}, u32[]{:S(2)}, u32[]{:S(2)}) collective-permute-start(f32[24,2,1,130]{3,2,1,0:T(1,128)S(1)} %get-tuple-element.225), channel_id=1, source_target_pairs={{1,0},{2,1},{3,2},{4,3},{5,4},{6,5},{7,6},{8,7},{9,8},{10,9},{11,1... | collective-permute-start | bytes 74888 | tf_op jit(solution)/shard_map/ppermute | solution.py:21
  448.2 10.9 %gather_fusion = f32[3072,24]{1,0:T(8,128)} fusion(f32[24,4096]{0,1:T(8,128)S(1)} %copy.38, s32[3072]{0:T(1024)S(1)} %broadcast_clamp_fusion), kind=kCustom, calls=%fused_computation.clone | custom fusion | bytes 602112 | tf_op jit(solution)/shard_map/jit(_take)/gather | solution.py:80
  464.8 10.9 %gather_fusion.1 = f32[3072,24]{1,0:T(8,128)} fusion(f32[24,4096]{0,1:T(8,128)S(1)} %bitcast.225, s32[3072]{0:T(1024)S(1)} %broadcast_clamp_fusion), kind=kCustom, calls=%fused_computation.1.clone | custom fusion | bytes 602112 | tf_op jit(solution)/shard_map/jit(_take)/gather | solution.py:81
  480.4 7.3 all-gather
  487.7 34.3 %all-reduce.12.cloned.1.call-done = (f32[24,384]{0,1:T(8,128)}, f32[24,384]{0,1:T(8,128)}) async-done(((f32[24,384]{0,1:T(8,128)}, f32[24,384]{0,1:T(8,128)}), (f32[24,384]{0,1:T(8,128)}, f32[24,384]{0,1:T(8,128)})) %all-reduce.12.cloned.1.call-update) | async-done | bytes 73744 | tf_op jit(solution)/shard_map/psum | solution.py:139
  522.2 298.9 %all-reduce.10.cloned.1.call-done = (f32[24,384]{0,1:T(8,128)}, f32[24,384]{0,1:T(8,128)}) async-done(((f32[24,384]{0,1:T(8,128)}, f32[24,384]{0,1:T(8,128)}), (f32[24,384]{0,1:T(8,128)}, f32[24,384]{0,1:T(8,128)})) %all-reduce.10.cloned.1.call-update) | async-done | bytes 73744 | tf_op jit(solution)/shard_map/psum | solution.py:139
  (236 shorter events, 284.5 us)
Async XLA Ops:
  34.5 17.9 %copy-start.11 = (bf16[9,64]{1,0:T(8,128)(2,1)S(1)}, bf16[9,64]{1,0:T(8,128)(2,1)}, u32[]{:S(2)}) copy-start(bf16[9,64]{1,0:T(8,128)(2,1)} %param.19) | copy-start | bytes 3460
  40.1 10.8 %collective-permute-start = (f32[6,2,1,512]{3,0,2,1:T(8,128)S(1)}, f32[6,2,1,512]{3,0,2,1:T(8,128)S(1)}, u32[]{:S(2)}, u32[]{:S(2)}) collective-permute-start(f32[6,2,1,512]{3,0,2,1:T(8,128)S(1)} %get-tuple-element.230), channel_id=1, source_target_pairs={{0,1},{1,2},{2,3},{3,4},{4,5},{5,6},{6,7},{7,8},{8,9},{9,10},{10,1... | collective-permute-start | bytes 73736 | tf_op jit(solution)/shard_map/ppermute | solution.py:19
  44.0 8.3 collective-permute-start.1
  88.0 22.1 %copy-start.19 = (s32[384,8]{0,1:T(8,128)S(1)}, s32[384,8]{0,1:T(8,128)}, u32[]{:S(2)}) copy-start(s32[384,8]{0,1:T(8,128)} %param.24) | copy-start | bytes 36868
  90.7 25.0 %collective-permute-start.2 = (bf16[6,2,64,1,512]{4,2,3,1,0:T(8,128)(2,1)}, bf16[6,2,64,1,512]{4,2,3,1,0:T(8,128)(2,1)S(1)}, u32[]{:S(2)}, u32[]{:S(2)}) collective-permute-start(bf16[6,2,64,1,512]{4,2,3,1,0:T(8,128)(2,1)} %get-tuple-element.222), channel_id=1, source_target_pairs={{0,1},{1,2},{2,3},{3,4},{4,5},{5,6},{6,7},{7,8},{8,9},{9,10},{10,1... | collective-permute-start | bytes 2359304 | tf_op jit(solution)/shard_map/ppermute | solution.py:19
  92.6 24.4 %collective-permute-start.3 = (bf16[6,2,64,1,512]{4,2,3,1,0:T(8,128)(2,1)}, bf16[6,2,64,1,512]{4,2,3,1,0:T(8,128)(2,1)S(1)}, u32[]{:S(2)}, u32[]{:S(2)}) collective-permute-start(bf16[6,2,64,1,512]{4,2,3,1,0:T(8,128)(2,1)} %get-tuple-element.223), channel_id=1, source_target_pairs={{1,0},{2,1},{3,2},{4,3},{5,4},{6,5},{7,6},{8,7},{9,8},{10,9},{11,1... | collective-permute-start | bytes 2359304 | tf_op jit(solution)/shard_map/ppermute | solution.py:21
  102.1 290.5 %collective-permute-start.7 = (f32[24,2,16,1]{3,2,1,0:T(8,128)}, f32[24,2,16,1]{3,2,1,0:T(8,128)}, u32[]{:S(2)}, u32[]{:S(2)}) collective-permute-start(f32[24,2,16,1]{3,2,1,0:T(8,128)} %broadcast_in_dim.48), channel_id=1, source_target_pairs={{0,32},{32,64},{64,96},{1,33},{33,65},{65,97},{2,34},{34,66},{66,9... | collective-permute-start | bytes 9224 | tf_op jit(solution)/shard_map/ppermute | solution.py:19
  104.9 287.8 %collective-permute-start.8 = (f32[24,2,16,1]{3,2,1,0:T(8,128)}, f32[24,2,16,1]{3,2,1,0:T(8,128)}, u32[]{:S(2)}, u32[]{:S(2)}) collective-permute-start(f32[24,2,16,1]{3,2,1,0:T(8,128)} %broadcast_in_dim.50), channel_id=1, source_target_pairs={{32,0},{64,32},{96,64},{33,1},{65,33},{97,65},{34,2},{66,34},{98,6... | collective-permute-start | bytes 9224 | tf_op jit(solution)/shard_map/ppermute | solution.py:21
  110.9 16.5 %copy-start.3 = (bf16[9,64,64]{2,1,0:T(8,128)(2,1)S(1)}, bf16[9,64,64]{2,1,0:T(8,128)(2,1)}, u32[]{:S(2)}) copy-start(bf16[9,64,64]{2,1,0:T(8,128)(2,1)} %param.20) | copy-start | bytes 221188
  110.9 16.5 %copy-start.18 = (bf16[64]{0:T(256)(128)(2,1)S(1)}, bf16[64]{0:T(256)(128)(2,1)}, u32[]{:S(2)}) copy-start(bf16[64]{0:T(256)(128)(2,1)} %param.21) | copy-start | bytes 388
  359.0 12.7 %all-to-all-start = ((f32[4,1,24576]{2,1,0:T(1,128)}), f32[4,1,24576]{2,1,0:T(1,128)S(1)}, u32[]{:S(2)}, u32[]{:S(2)}) async-start(f32[4,1,24576]{2,1,0:T(1,128)} %reshape.341), calls=%async_computation | async-start | bytes 786432 | tf_op jit(solution)/shard_map/all_to_all | solution.py:115
  365.9 156.1 %all-reduce.12.cloned.1.call-start = ((), (), s32[]{:S(2)}) async-start(), calls=%async_computation.2 | async-start | bytes 786432 | tf_op jit(solution)/shard_map/psum | solution.py:139
  385.6 18.8 %collective-permute-start.4 = (f32[24,2,16,1]{3,2,1,0:T(8,128)S(1)}, f32[24,2,16,1]{3,2,1,0:T(8,128)S(1)}, u32[]{:S(2)}, u32[]{:S(2)}) collective-permute-start(f32[24,2,16,1]{3,2,1,0:T(8,128)S(1)} %get-tuple-element.234), channel_id=1, source_target_pairs={{0,32},{32,64},{64,96},{1,33},{33,65},{65,97},{2,34},{34,66},{66,9... | collective-permute-start | bytes 9224 | tf_op jit(solution)/shard_map/ppermute | solution.py:19
  387.5 16.9 %collective-permute-start.5 = (f32[24,2,16,1]{3,2,1,0:T(8,128)S(1)}, f32[24,2,16,1]{3,2,1,0:T(8,128)S(1)}, u32[]{:S(2)}, u32[]{:S(2)}) collective-permute-start(f32[24,2,16,1]{3,2,1,0:T(8,128)S(1)} %get-tuple-element.235), channel_id=1, source_target_pairs={{32,0},{64,32},{96,64},{33,1},{65,33},{97,65},{34,2},{66,34},{98,6... | collective-permute-start | bytes 9224 | tf_op jit(solution)/shard_map/ppermute | solution.py:21
  394.3 20.6 %collective-permute-start.11 = (f32[24,2,1,130]{3,2,1,0:T(1,128)S(1)}, f32[24,2,1,130]{3,2,1,0:T(1,128)S(1)}, u32[]{:S(2)}, u32[]{:S(2)}) collective-permute-start(f32[24,2,1,130]{3,2,1,0:T(1,128)S(1)} %get-tuple-element.228), channel_id=1, source_target_pairs={{0,1},{1,2},{2,3},{3,4},{4,5},{5,6},{6,7},{7,8},{8,9},{9,10},{10,1... | collective-permute-start | bytes 74888 | tf_op jit(solution)/shard_map/ppermute | solution.py:19
  396.3 18.6 %collective-permute-start.9 = (f32[24,2,1,130]{3,2,1,0:T(1,128)S(1)}, f32[24,2,1,130]{3,2,1,0:T(1,128)S(1)}, u32[]{:S(2)}, u32[]{:S(2)}) collective-permute-start(f32[24,2,1,130]{3,2,1,0:T(1,128)S(1)} %get-tuple-element.229), channel_id=1, source_target_pairs={{1,0},{2,1},{3,2},{4,3},{5,4},{6,5},{7,6},{8,7},{9,8},{10,9},{11,1... | collective-permute-start | bytes 74888 | tf_op jit(solution)/shard_map/ppermute | solution.py:21
  404.8 11.9 %collective-permute-start.10 = (f32[24,2,1,130]{3,2,1,0:T(1,128)S(1)}, f32[24,2,1,130]{3,2,1,0:T(1,128)S(1)}, u32[]{:S(2)}, u32[]{:S(2)}) collective-permute-start(f32[24,2,1,130]{3,2,1,0:T(1,128)S(1)} %get-tuple-element.226), channel_id=1, source_target_pairs={{0,1},{1,2},{2,3},{3,4},{4,5},{5,6},{6,7},{7,8},{8,9},{9,10},{10,1... | collective-permute-start | bytes 74888 | tf_op jit(solution)/shard_map/ppermute | solution.py:19
  406.7 9.9 %collective-permute-start.6 = (f32[24,2,1,130]{3,2,1,0:T(1,128)S(1)}, f32[24,2,1,130]{3,2,1,0:T(1,128)S(1)}, u32[]{:S(2)}, u32[]{:S(2)}) collective-permute-start(f32[24,2,1,130]{3,2,1,0:T(1,128)S(1)} %get-tuple-element.227), channel_id=1, source_target_pairs={{1,0},{2,1},{3,2},{4,3},{5,4},{6,5},{7,6},{8,7},{9,8},{10,9},{11,1... | collective-permute-start | bytes 74888 | tf_op jit(solution)/shard_map/ppermute | solution.py:21
  422.4 10.6 %collective-permute-start.12 = (f32[24,2,16,1]{3,2,1,0:T(8,128)S(1)}, f32[24,2,16,1]{3,2,1,0:T(8,128)S(1)}, u32[]{:S(2)}, u32[]{:S(2)}) collective-permute-start(f32[24,2,16,1]{3,2,1,0:T(8,128)S(1)} %get-tuple-element.232), channel_id=1, source_target_pairs={{0,32},{32,64},{64,96},{1,33},{33,65},{65,97},{2,34},{34,66},{66,9... | collective-permute-start | bytes 9224 | tf_op jit(solution)/shard_map/ppermute | solution.py:19
  424.3 10.4 %collective-permute-start.13 = (f32[24,2,16,1]{3,2,1,0:T(8,128)S(1)}, f32[24,2,16,1]{3,2,1,0:T(8,128)S(1)}, u32[]{:S(2)}, u32[]{:S(2)}) collective-permute-start(f32[24,2,16,1]{3,2,1,0:T(8,128)S(1)} %get-tuple-element.233), channel_id=1, source_target_pairs={{32,0},{64,32},{96,64},{33,1},{65,33},{97,65},{34,2},{66,34},{98,6... | collective-permute-start | bytes 9224 | tf_op jit(solution)/shard_map/ppermute | solution.py:21
  435.1 24.0 %collective-permute-start.14 = (f32[24,2,1,130]{3,2,1,0:T(1,128)S(1)}, f32[24,2,1,130]{3,2,1,0:T(1,128)S(1)}, u32[]{:S(2)}, u32[]{:S(2)}) collective-permute-start(f32[24,2,1,130]{3,2,1,0:T(1,128)S(1)} %get-tuple-element.225), channel_id=1, source_target_pairs={{1,0},{2,1},{3,2},{4,3},{5,4},{6,5},{7,6},{8,7},{9,8},{10,9},{11,1... | collective-permute-start | bytes 74888 | tf_op jit(solution)/shard_map/ppermute | solution.py:21
  443.5 15.6 %collective-permute-start.15 = (f32[24,2,1,130]{3,2,1,0:T(1,128)S(1)}, f32[24,2,1,130]{3,2,1,0:T(1,128)S(1)}, u32[]{:S(2)}, u32[]{:S(2)}) collective-permute-start(f32[24,2,1,130]{3,2,1,0:T(1,128)S(1)} %get-tuple-element.224), channel_id=1, source_target_pairs={{0,1},{1,2},{2,3},{3,4},{4,5},{5,6},{6,7},{7,8},{8,9},{9,10},{10,1... | collective-permute-start | bytes 74888 | tf_op jit(solution)/shard_map/ppermute | solution.py:19
  475.7 46.4 %copy-start.16 = (f32[24,384]{1,0:T(8,128)S(1)}, f32[24,384]{1,0:T(8,128)}, u32[]{:S(2)}) copy-start(f32[24,384]{1,0:T(8,128)} %param.26) | copy-start | bytes 110596
  480.4 340.8 %all-reduce.10.cloned.1.call-start = ((), (), s32[]{:S(2)}) async-start(), calls=%async_computation.1 | async-start | bytes 786432 | tf_op jit(solution)/shard_map/psum | solution.py:139
  (18 other events, 144.7 us)
Sparse Core Ops, SparseCore 0:
  480.5 41.4 all-reduce.11
  524.7 296.3 all-reduce.9
